TPU v7x, 32 devices: a whole 2x2x4 slice. The times are simulated.
32 devices in a mesh: clip: 2 (over y), tile: 4 (over z), tm: 2 (over x), chan: 2 (over core).
Axes of the slice: x: 2, y: 2, z: 4, core: 2. Of those that a mesh axis runs over, the one named last changes fastest.
Arguments:
- latent: bfloat16 [8, 8, 256, 128], P(('clip', 'tm'), 'tile', 'chan'), parts along dimension 0
- norm1_gain: float32 [256], P('chan'), may hold values from 0.25 to 1.75
- norm1_bias: float32 [256], P('chan'), may hold values from -3 to 3
- conv1_weight: bfloat16 [3, 3, 3, 256, 256], P(None, None, None, None, 'chan'), may hold values from -0.078125 to 0.078125
- conv1_bias: float32 [256], P('chan'), may hold values from -3 to 3
- norm2_gain: float32 [256], P('chan'), may hold values from 0.25 to 1.75
- norm2_bias: float32 [256], P('chan'), may hold values from -3 to 3
- conv2_weight: bfloat16 [3, 3, 3, 256, 256], P(None, None, None, None, 'chan'), may hold values from -0.078125 to 0.078125
- conv2_bias: float32 [256], P('chan'), may hold values from -3 to 3
Outputs:
- upsampled: bfloat16 [8, 16, 64, 256], P(('clip', 'tm'), 'tile', 'chan'), parts along dimension 0
There are 2 independent parts, one for each index of `clip`. A program takes and returns all parts, laid end to end along the dimension named above; an argument that names none is the same for every part. Nothing has to cross between parts.
All inputs are finite; a program needn't handle non-finite values.
Results may differ from a plain program's by a relative error of at most 0.0026.
Values may be sent and summed in bfloat16 or wider, within the bound.
A program may use at most 64 MiB of HBM per device.

v0:
```python
import functools

import jax
import jax.numpy as jnp
from jax import lax
from jax.experimental import pallas as pl
from jax.experimental.pallas import tpu as pltpu
from jax.sharding import PartitionSpec as P

MESH = pl.DeviceIdType.MESH
C = 256
GROUPS = 32
SIZE = C // GROUPS
F32 = jnp.float32
BF16 = jnp.bfloat16


def iota(shape, dim):
    return lax.broadcasted_iota(jnp.int32, shape, dim)


def column(row, n):
    wide = jnp.broadcast_to(row, (n, row.shape[-1]))
    return jnp.sum(jnp.where(iota(wide.shape, 0) == iota(wide.shape, 1), wide, 0.0), axis=1, keepdims=True)


def kernel(
    tiles,
    blocks,
    latent,
    n1g,
    n1b,
    w1,
    c1b,
    n2g,
    n2b,
    w2,
    c2b,
    out,
    w1v,
    w2v,
    w1t,
    w2t,
    lat,
    act1,
    hid,
    act2,
    mix,
    select,
    params,
    own_stats,
    stats,
    means,
    scales,
    l_sem,
    w_sem,
    p_sem,
    x_send,
    z_send,
    d_send,
    a_recv,
    d_recv,
    hz_send,
    hd_send,
    h_recv,
    hd_recv,
    s_send,
    s_recv,
):
    cores = 2
    count_all = tiles * blocks * cores
    tm = lax.axis_index("tm")
    tile = lax.axis_index("tile")
    core = lax.axis_index("chan")
    other = 1 - core
    me = (tm * cores + core) * tiles + tile
    local = latent.shape[2]
    wide = latent.shape[3]
    groups = local // SIZE
    rows = latent.shape[1]

    def where_is(index):
        return {"tm": index // (cores * tiles), "chan": (index // tiles) % cores, "tile": index % tiles}

    def remote(src, dst, send, recv, **device):
        return pltpu.make_async_remote_copy(
            src_ref=src, dst_ref=dst, send_sem=send, recv_sem=recv, device_id=device, device_id_type=MESH
        )

    loads = [pltpu.make_async_copy(latent.at[:, r], lat.at[2, 1 + r, core], l_sem.at[r]) for r in (0, 1)]
    loads += [
        pltpu.make_async_copy(ref, params.at[core, i], l_sem.at[2 + i])
        for i, ref in enumerate((n1g, n1b, n2g, n2b, c1b, c2b))
    ]
    load1 = pltpu.make_async_copy(w1, w1v, w_sem.at[0])
    load2 = pltpu.make_async_copy(w2, w2v, w_sem.at[1])
    barrier = pltpu.get_barrier_semaphore()

    def greet(step, carry):
        pl.semaphore_signal(
            barrier, inc=1, device_id=where_is(lax.rem(me + step, count_all)), device_id_type=MESH
        )
        return carry

    lax.fori_loop(1, count_all, greet, 0)
    for copy in loads:
        copy.start()
    load1.start()
    load2.start()
    for copy in loads:
        copy.wait()

    started = []

    def go(condition, copy):
        @pl.when(condition)
        def _():
            copy.start()

        started.append((condition, copy))

    always = core >= 0
    has_up = tile < tiles - 1
    has_down = tile > 0
    slots = [s for s in range(3) if blocks > 2 - s]
    before = [s for s in slots if s < 2]

    def lat_copy(s, row, f, to_s, to_row, send, recv, **device):
        return remote(lat.at[s, row, core, f], lat.at[to_s, to_row, core, f], send, recv, **device)

    lanes = iota((groups, 128), 1)
    subs = iota((groups, 128), 0)

    def make_stats(which, field):
        row = jnp.zeros((1, 128), F32)
        for f in (0, 1):
            total = jnp.zeros((groups, wide), F32)
            square = jnp.zeros((groups, wide), F32)
            for r in (0, 1):
                v = field(f, r).reshape(groups, SIZE, wide)
                total = total + jnp.sum(v, axis=1)
                square = square + jnp.sum(v * v, axis=1)
            for kind, part in enumerate((total, square)):
                col = jnp.sum(part, axis=1, keepdims=True)
                at = kind * 2 * groups + f * groups
                row = row + jnp.sum(jnp.where(lanes == subs + at, col, 0.0), axis=0, keepdims=True)
        own_stats[which] = row
        stats[which, me] = row

    def send_stats(which):
        def send(step, carry):
            to = lax.rem(me + step, count_all)
            remote(own_stats.at[which], stats.at[which, me], s_send.at[which, to], s_recv.at[which, me],
                   **where_is(to)).start()
            return carry

        lax.fori_loop(1, count_all, send, 0)

    def wait_stats(which):
        def wait(step, carry):
            to = lax.rem(me + step, count_all)
            remote(own_stats.at[which], stats.at[which, to], s_send.at[which, to], s_recv.at[which, to],
                   **where_is(to)).wait()
            return carry

        lax.fori_loop(1, count_all, wait, 0)

    def make_norms(which, frames):
        ahead = frames // 2 - 1
        per_block = []
        for b in range(blocks):
            for c in range(cores):
                first = jnp.sum(stats[which, pl.ds((b * cores + c) * tiles, tiles)], axis=0)
                both = first + pltpu.roll(first, 128 - groups, 1)
                per_block.append((b, c, first, both))
        for e in range(frames):
            block = tm - ahead + e // 2
            later = jnp.logical_and(block >= 0, e % 2 == 1)
            block = jnp.maximum(block, 0)
            number = (block * 2 + later.astype(jnp.int32) + 1).astype(F32)
            count = number * float(rows * tiles * SIZE * wide)
            for c in range(cores):
                run = jnp.zeros((1, 128), F32)
                for b, cc, first, both in per_block:
                    if cc == c:
                        whole = jnp.logical_or(b < block, jnp.logical_and(b == block, later))
                        run = run + jnp.where(whole, both, jnp.where(b == block, first, 0.0))
                mean = run / count
                var = pltpu.roll(mean, 128 - 2 * groups, 1) - mean * mean
                scale = 1.0 / jnp.sqrt(var + 1e-06)
                diagonal = lanes == subs
                for ref, value in ((means, mean), (scales, scale)):
                    col = jnp.sum(jnp.where(diagonal, jnp.broadcast_to(value, lanes.shape), 0.0), axis=1,
                                  keepdims=True)
                    ref[e * cores + c] = jnp.broadcast_to(col, (groups, 128))

    def per_channel(ref, at):
        v = ref[at]
        return jnp.broadcast_to(v[:, None, :], (groups, SIZE, 128)).reshape(local, 128)

    def flip(src, dst):
        def one(j, carry):
            for i in range(3):
                for k in range(3):
                    dst[j, k * local:(k + 1) * local, i * C:(i + 1) * C] = src[i, j, k].T
            return carry

        lax.fori_loop(0, 3, one, 0)

    def silu_of_twice(half):
        return half + half * jnp.tanh(half)

    def clear_edges(act):
        for side, row in ((has_down, 0), (has_up, 3)):
            @pl.when(jnp.logical_not(side))
            def _(row=row):
                act[:, row * wide:(row + 1) * wide] = jnp.zeros((act.shape[0], wide), BF16)

    def conv(act, wt, o):
        acc = None
        for j in range(3):
            part = jnp.dot(
                wt[j], act[pl.ds(pl.multiple_of(o * C, C), 3 * C), j * wide:(j + 2) * wide],
                preferred_element_type=F32,
            )
            acc = part if acc is None else acc + part
        lane = iota((local, wide), 1)
        result = []
        for r in range(2):
            a = [acc[k * local:(k + 1) * local, r * wide:(r + 1) * wide] for k in range(3)]
            left = jnp.where(lane == 0, 0.0, pltpu.roll(a[0], 1, 1))
            right = jnp.where(lane == wide - 1, 0.0, pltpu.roll(a[2], wide - 1, 1))
            result.append(a[1] + left + right)
        return result

    make_stats(0, lambda f, r: lat[2, 1 + r, core, f].astype(F32))
    pl.semaphore_wait(barrier, count_all - 1)
    send_stats(0)

    for s in reversed(before):
        for f in (0, 1):
            for r in (0, 1):
                go(tm + (2 - s) < blocks,
                   lat_copy(2, 1 + r, f, s, 1 + r, x_send.at[s, r, f], a_recv.at[s, 1 + r, f], tm=tm + (2 - s)))
    for f in (0, 1):
        go(has_up, lat_copy(2, 2, f, 2, 0, z_send.at[2, 0, f], a_recv.at[2, 0, f], tile=tile + 1))
        go(has_down, lat_copy(2, 1, f, 2, 3, z_send.at[2, 1, f], a_recv.at[2, 3, f], tile=tile - 1))
    for f in (0, 1):
        for r in (1, 2):
            go(always, lat_copy(2, r, f, 2, r, d_send.at[2, r, f], d_recv.at[2, r, f], chan=other))
    go(always, remote(params.at[core], params.at[core], p_sem.at[0], p_sem.at[1], chan=other))

    a, b = iota((2 * wide, 2 * wide), 0), iota((2 * wide, 2 * wide), 1)
    select[...] = jnp.where(b == 2 * (a % wide) + a // wide, 1.0, 0.0).astype(BF16)
    load1.wait()
    flip(w1v, w1t)
    load2.wait()
    flip(w2v, w2t)

    def arrived(s, row, f, condition):
        copy = lat_copy(s, row, f, s, row, d_send.at[s, row, f], d_recv.at[s, row, f], chan=other)

        @pl.when(condition)
        def _():
            lat_copy(s, row, f, s, row, d_send.at[s, row, f], a_recv.at[s, row, f], chan=other).wait_recv()
            copy.start()

        started.append((condition, copy))

    def from_other(s, row, f, condition):
        @pl.when(condition)
        def _():
            remote(lat.at[s, row, core, f], lat.at[s, row, other, f], d_send.at[s, row, f], d_recv.at[s, row, f],
                   chan=other).wait_recv()

    def row_here(row):
        return has_down if row == 0 else has_up if row == 3 else always

    for s in reversed(before):
        here = tm >= 2 - s
        for f in (0, 1):
            for r in (0, 1):
                arrived(s, 1 + r, f, here)
                side, row, to = ((has_down, 3, tile - 1), (has_up, 0, tile + 1))[r]
                go(jnp.logical_and(here, side),
                   lat_copy(s, 1 + r, f, s, row, z_send.at[s, 1 - r, f], a_recv.at[s, row, f], tile=to))

    for f in (0, 1):
        for row in (0, 3):
            arrived(2, row, f, row_here(row))

    wait_stats(0)
    make_norms(0, 6)
    remote(params.at[core], params.at[other], p_sem.at[0], p_sem.at[1], chan=other).wait_recv()
    for f in (0, 1):
        for row in range(4):
            from_other(2, row, f, row_here(row))

    def norm1(first, rows_of):
        def one(step, carry):
            e, c = step // cores, step % cores
            s, f = e // 2, e % 2
            f = jnp.where(tm - 2 + s < 0, 0, f)
            s = jnp.maximum(s, 2 - tm)
            gain = per_channel(scales, step) * column(0.5 * params[c, 0], local)
            bias = column(0.5 * params[c, 1], local) - per_channel(means, step) * gain
            for row in rows_of:
                v = silu_of_twice(lat[s, row, c, f].astype(F32) * gain + bias)
                act1[pl.ds(pl.multiple_of(step * local, local), local), row * wide:(row + 1) * wide] = v.astype(BF16)
            return carry

        lax.fori_loop(first * cores, (first + 2) * cores, one, 0)

    norm1(4, range(4))
    for s in before:
        for f in (0, 1):
            for row in (0, 3):
                arrived(s, row, f, jnp.logical_and(tm >= 2 - s, row_here(row)))
    for s in before:
        for f in (0, 1):
            for row in (1, 2):
                from_other(s, row, f, tm >= 2 - s)
    norm1(2, (1, 2))
    for s in before:
        for f in (0, 1):
            for row in (0, 3):
                from_other(s, row, f, jnp.logical_and(tm >= 2 - s, row_here(row)))
    norm1(2, (0, 3))

    def repeat_first():
        first = act1[2 * C:3 * C]
        act1[0:C] = first
        act1[C:2 * C] = first

    if blocks > 2:
        @pl.when(tm >= 2)
        def _():
            norm1(0, range(4))

        pl.when(tm < 2)(repeat_first)
    else:
        repeat_first()

    clear_edges(act1)

    def z_copy(o, up):
        at, row, to, landed = (0, 2, tile + 1, 0) if up else (1, 1, tile - 1, 3)
        return remote(hid.at[row, core, o], hid.at[landed, core, o], hz_send.at[at, o], h_recv.at[at, o], tile=to)

    def d_copy(o, row):
        return remote(hid.at[row, core, o], hid.at[row, core, o], hd_send.at[row, o], hd_recv.at[row, o], chan=other)

    def conv1(o, carry):
        for r, h in enumerate(conv(act1, w1t, o)):
            hid[1 + r, core, o] = h.astype(BF16)

            @pl.when(o >= 2)
            def _():
                mix[jnp.maximum(o - 2, 0) * 2 + r] = h

        pl.when(has_up)(lambda: z_copy(o, True).start())
        pl.when(has_down)(lambda: z_copy(o, False).start())
        d_copy(o, 1).start()
        d_copy(o, 2).start()
        return carry

    lax.fori_loop(2, 4, conv1, 0)
    bias1 = column(params[core, 4], local)
    make_stats(1, lambda f, r: mix[f * 2 + r] + bias1)
    send_stats(1)
    lax.fori_loop(0, 2, conv1, 0)

    for o in (2, 3, 0, 1):
        for at, row in ((0, 0), (1, 3)):
            @pl.when(row_here(row))
            def _(at=at, row=row, o=o):
                remote(hid.at[row, core, o], hid.at[row, core, o], hd_send.at[row, o], h_recv.at[at, o],
                       chan=other).wait_recv()
                d_copy(o, row).start()
    wait_stats(1)
    make_norms(1, 4)

    def got(o, row):
        remote(hid.at[row, core, o], hid.at[row, other, o], hd_send.at[row, o], hd_recv.at[row, o],
               chan=other).wait_recv()

    def norm2(rows_of, step, carry):
        e, c = step // cores, step % cores
        gain = per_channel(scales, step) * column(0.5 * params[c, 2], local)
        bias = column(0.5 * params[c, 3], local) + (column(params[c, 4], local) - per_channel(means, step)) * gain
        for row in rows_of:
            v = silu_of_twice(hid[row, c, e].astype(F32) * gain + bias)
            act2[pl.ds(pl.multiple_of(step * local, local), local), row * wide:(row + 1) * wide] = v.astype(BF16)
        return carry

    for o in (2, 3, 0, 1):
        got(o, 1)
        got(o, 2)
    lax.fori_loop(0, 4 * cores, functools.partial(norm2, (1, 2)), 0)
    for o in (2, 3, 0, 1):
        pl.when(has_down)(lambda o=o: got(o, 0))
        pl.when(has_up)(lambda o=o: got(o, 3))
    lax.fori_loop(0, 4 * cores, functools.partial(norm2, (0, 3)), 0)
    clear_edges(act2)

    bias2 = column(params[core, 5], local)

    def conv2(o, carry):
        for r, h in enumerate(conv(act2, w2t, o)):
            mix[o * 2 + r] = lat[2, 1 + r, core, o].astype(F32) + (h + bias2)
        return carry

    lax.fori_loop(0, 2, conv2, 0)

    spread = select[...]
    for f in range(2):
        for r in range(2):
            for p in range(2):
                pair = [mix[f * 2 + r, pl.ds(2 * p + q, local // 4, stride=4), :].astype(BF16) for q in range(2)]
                out[f, 2 * r + p] = jnp.dot(
                    jnp.concatenate(pair, axis=1), spread, preferred_element_type=F32
                ).astype(BF16)

    for condition, copy in started:
        @pl.when(condition)
        def _(copy=copy):
            copy.wait_send()

    for o in range(4):
        pl.when(has_up)(lambda o=o: z_copy(o, True).wait_send())
        pl.when(has_down)(lambda o=o: z_copy(o, False).wait_send())
        for row in range(4):
            pl.when(row_here(row))(lambda o=o, row=row: d_copy(o, row).wait_send())


def shards(tiles, blocks, latent, n1g, n1b, w1, c1b, n2g, n2b, w2, c2b):
    frames, rows, local, wide = latent.shape
    count = tiles * blocks * 2
    groups = local // SIZE
    vmem = pl.BlockSpec(memory_space=pltpu.VMEM)
    hbm = pl.BlockSpec(memory_space=pl.ANY)
    dma = pltpu.SemaphoreType.DMA
    here = lambda v: pltpu.with_memory_space_constraint(v, pltpu.HBM)
    row = lambda v: here(v.reshape(1, local))
    return pl.pallas_call(
        functools.partial(kernel, tiles, blocks),
        out_shape=jax.ShapeDtypeStruct((frames, 2 * rows, local // 4, 2 * wide), BF16),
        in_specs=[hbm] * 9,
        out_specs=vmem,
        scratch_shapes=[
            pltpu.VMEM(w1.shape, BF16),
            pltpu.VMEM(w2.shape, BF16),
            pltpu.VMEM((3, 3 * local, 3 * C), BF16),
            pltpu.VMEM((3, 3 * local, 3 * C), BF16),
            pltpu.VMEM((3, 4, 2, 2, local, wide), BF16),
            pltpu.VMEM((6 * C, 4 * wide), BF16),
            pltpu.VMEM((4, 2, 4, local, wide), BF16),
            pltpu.VMEM((4 * C, 4 * wide), BF16),
            pltpu.VMEM((4, local, wide), F32),
            pltpu.VMEM((2 * wide, 2 * wide), BF16),
            pltpu.VMEM((2, 6, 1, local), F32),
            pltpu.VMEM((2, 1, 128), F32),
            pltpu.VMEM((2, count, 1, 128), F32),
            pltpu.VMEM((12, groups, 128), F32),
            pltpu.VMEM((12, groups, 128), F32),
            dma((8,)),
            dma((2,)),
            dma((2,)),
            dma((2, 2, 2)),
            dma((3, 2, 2)),
            dma((3, 4, 2)),
            dma((3, 4, 2)),
            dma((3, 4, 2)),
            dma((2, 4)),
            dma((4, 4)),
            dma((2, 4)),
            dma((4, 4)),
            dma((2, count)),
            dma((2, count)),
        ],
        compiler_params=pltpu.CompilerParams(
            collective_id=0, has_side_effects=True, vmem_limit_bytes=48 * 1024 * 1024
        ),
        name="block",
    )(here(latent), row(n1g), row(n1b), here(w1), row(c1b), row(n2g), row(n2b), here(w2), row(c2b))


def solution(mesh):
    return jax.shard_map(
        functools.partial(shards, mesh.shape["tile"], mesh.shape["tm"]),
        mesh=mesh,
        in_specs=(
            P(("clip", "tm"), "tile", "chan", None),
            P("chan"),
            P("chan"),
            P(None, None, None, None, "chan"),
            P("chan"),
            P("chan"),
            P("chan"),
            P(None, None, None, None, "chan"),
            P("chan"),
        ),
        out_specs=P(("clip", "tm"), "tile", "chan", None),
        check_vma=False,
    )
```

profile of v0, /device:TPU:3, one launch (start us, length us, event | category | flops | bytes accessed | tf_op | source)
XLA Modules:
  0.0 27.4 jit_solution(8373402654537232963)
XLA Ops:
  0.0 26.7 %block.1 = bf16[2,4,32,256]{3,2,1,0:T(8,128)(2,1)S(1)} custom-call(bf16[2,2,128,128]{3,2,1,0:T(8,128)(2,1)} %latent.1, f32[1,128]{1,0:T(1,128)} %bitcast.6, f32[1,128]{1,0:T(1,128)} %bitcast.7, bf16[3,3,3,256,128]{4,3,2,1,0:T(8,128)(2,1)} %w1.1, f32[1,128]{1,0:T(1,128)} %bitcast.8, f32[1,128]{1,0:T(1,128)} %bitcast.9, f32[1,128]{1,0:T(1,128)} %bitcast.10, ...), custom_call_target="tpu_custom_call" | custom-call | tf_op jit(solution)/shard_map/block/pallas_call | solution.py:445
  26.8 0.7 %copy.11 = bf16[2,4,32,256]{3,2,1,0:T(8,128)(2,1)} copy(bf16[2,4,32,256]{3,2,1,0:T(8,128)(2,1)S(1)} %block.1) | data formatting | bytes 262144
where the time goes:
time: 27.6 us; the launch traced here: 27.4 us
  Pallas kernels  26.7 us (97%)
  local copies, waits for them, and re-layouts  0.66 us (2%)
    pallas_call x1, Pallas kernels, shards(): pl.pallas_call(functools.partial(kernel, tiles, blocks), out_shape=jax.Sh...  26.7 us
    unnamed x1, local copies, waits for them, and re-layouts  0.66 us

commit v1 on v0

v1 whole, which is shorter than its diff:
```python
import functools

import jax
import jax.numpy as jnp
from jax import lax
from jax.experimental import pallas as pl
from jax.experimental.pallas import tpu as pltpu
from jax.sharding import PartitionSpec as P

MESH = pl.DeviceIdType.MESH
C = 256
GROUPS = 32
SIZE = C // GROUPS
F32 = jnp.float32
BF16 = jnp.bfloat16


def iota(shape, dim):
    return lax.broadcasted_iota(jnp.int32, shape, dim)


def column(row, n):
    wide = jnp.broadcast_to(row, (n, row.shape[-1]))
    return jnp.sum(jnp.where(iota(wide.shape, 0) == iota(wide.shape, 1), wide, 0.0), axis=1, keepdims=True)


def kernel(
    tiles,
    blocks,
    latent,
    n1g,
    n1b,
    w1,
    c1b,
    n2g,
    n2b,
    w2,
    c2b,
    out,
    w1v,
    w2v,
    w1t,
    w2t,
    lat,
    act1,
    hid,
    hsend,
    hedge,
    act2,
    mix,
    select,
    params,
    cols,
    affine,
    own_stats,
    stats,
    l_sem,
    w_sem,
    x_send,
    z_send,
    a_recv,
    d_send,
    d_recv,
    hz_send,
    h_recv,
    e_send,
    e_recv,
    s_send,
    s_recv,
):
    tm = lax.axis_index("tm")
    tile = lax.axis_index("tile")
    core = lax.axis_index("chan")
    other = 1 - core
    me = tm * tiles + tile
    local = latent.shape[2]
    wide = latent.shape[3]
    groups = local // SIZE
    rows = latent.shape[1]

    def remote(src, dst, send, recv, **device):
        return pltpu.make_async_remote_copy(
            src_ref=src, dst_ref=dst, send_sem=send, recv_sem=recv, device_id=device, device_id_type=MESH
        )

    def when(condition, action):
        @pl.when(condition)
        def _():
            action()

    def each_peer(b, action):
        def one(t, carry):
            when(jnp.logical_or(t != tile, b != tm), lambda: action(t))
            return carry

        lax.fori_loop(0, tiles, one, 0)

    barrier = pltpu.get_barrier_semaphore()
    pl.semaphore_signal(barrier, inc=1, device_id={"chan": other}, device_id_type=MESH)
    for b in range(blocks):
        each_peer(b, lambda t, b=b: pl.semaphore_signal(
            barrier, inc=1, device_id={"tm": b, "tile": t}, device_id_type=MESH))

    loads = [pltpu.make_async_copy(latent, lat.at[2, :, 1:3], l_sem.at[0])]
    loads += [
        pltpu.make_async_copy(ref, params.at[i], l_sem.at[1 + i])
        for i, ref in enumerate((n1g, n1b, n2g, n2b, c1b, c2b))
    ]
    load1 = pltpu.make_async_copy(w1, w1v, w_sem.at[0])
    load2 = pltpu.make_async_copy(w2, w2v, w_sem.at[1])
    for copy in loads:
        copy.start()
    load1.start()
    load2.start()

    started = []

    def go(condition, copy):
        @pl.when(condition)
        def _():
            copy.start()

        started.append((condition, copy))

    always = core >= 0
    has_up = tile < tiles - 1
    has_down = tile > 0
    slots = [s for s in range(3) if blocks > 2 - s]
    before = [s for s in slots if s < 2]

    def row_here(row):
        return has_down if row == 0 else has_up if row == 3 else always

    def lat_copy(src, s, row, f, send, **device):
        return remote(src, lat.at[s, f, row], send, a_recv.at[s, row, f], **device)

    lanes = iota((groups, 128), 1)
    subs = iota((groups, 128), 0)

    def make_stats(which, field):
        row = jnp.zeros((1, 128), F32)
        for f in (0, 1):
            total = jnp.zeros((groups, wide), F32)
            square = jnp.zeros((groups, wide), F32)
            for r in (0, 1):
                v = field(f, r).reshape(groups, SIZE, wide)
                total = total + jnp.sum(v, axis=1)
                square = square + jnp.sum(v * v, axis=1)
            for kind, part in enumerate((total, square)):
                col = jnp.sum(part, axis=1, keepdims=True)
                at = kind * 2 * groups + f * groups
                row = row + jnp.sum(jnp.where(lanes == subs + at, col, 0.0), axis=0, keepdims=True)
        own_stats[which] = row
        stats[which, me] = row

    def stats_to(which, b, t):
        return remote(own_stats.at[which], stats.at[which, me], s_send.at[which, b * tiles + t],
                      s_recv.at[which, me], tm=b, tile=t)

    def send_stats(which):
        for b in range(blocks):
            when(b >= tm, lambda b=b: each_peer(b, lambda t: stats_to(which, b, t).start()))

    def wait_stats(which):
        for b in range(blocks):
            when(b <= tm, lambda b=b: each_peer(b, lambda t: remote(
                own_stats.at[which], stats.at[which, b * tiles + t], s_send.at[which, b * tiles + t],
                s_recv.at[which, b * tiles + t], tm=b, tile=t).wait_recv()))

    def make_norms(which, first_frame, frames, gain, bias, shift):
        ahead = frames // 2 - 1
        per_block = []
        for b in range(blocks):
            first = jnp.sum(stats[which, pl.ds(b * tiles, tiles)], axis=0)
            both = first + pltpu.roll(first, 128 - groups, 1)
            per_block.append((b, first, both))
        for e in range(first_frame, frames):
            block = tm - ahead + e // 2
            later = jnp.logical_and(block >= 0, e % 2 == 1)
            block = jnp.maximum(block, 0)
            number = (block * 2 + later.astype(jnp.int32) + 1).astype(F32)
            count = number * float(rows * tiles * SIZE * wide)
            run = jnp.zeros((1, 128), F32)
            for b, first, both in per_block:
                whole = jnp.logical_or(b < block, jnp.logical_and(b == block, later))
                run = run + jnp.where(whole, both, jnp.where(b == block, first, 0.0))
            mean = run / count
            var = pltpu.roll(mean, 128 - 2 * groups, 1) - mean * mean
            scale = 1.0 / jnp.sqrt(var + 1e-06)
            diagonal = lanes == subs

            def spread_out(value):
                col = jnp.sum(jnp.where(diagonal, jnp.broadcast_to(value, lanes.shape), 0.0), axis=1, keepdims=True)
                return jnp.broadcast_to(col[:, :, None], (groups, SIZE, 128)).reshape(local, 128)

            slope = spread_out(scale) * cols[gain]
            offset = -spread_out(mean)
            if shift is not None:
                offset = offset + cols[shift]
            affine[e, 0] = slope
            affine[e, 1] = cols[bias] + offset * slope

    def flip(src, dst):
        def one(j, carry):
            for i in range(3):
                for k in range(3):
                    dst[j, k * local:(k + 1) * local, i * C:(i + 1) * C] = src[i, j, k].T
            return carry

        lax.fori_loop(0, 3, one, 0)

    def silu_of_twice(half):
        return half + half * jnp.tanh(half)

    def part_of(act, row, e, which):
        return act.at[row, pl.ds(pl.multiple_of(e * C + which * local, local), local)]

    def normed(act, send, recv, e, row, value):
        v = silu_of_twice(value * affine[e, 0] + affine[e, 1])
        mine = part_of(act, row, e, core)
        mine[...] = v.astype(BF16)
        remote(mine, mine, send.at[row, e], recv.at[row, e], chan=other).start()

    def of_other(act, send, recv, e, row):
        return remote(part_of(act, row, e, core), part_of(act, row, e, other), send.at[row, e], recv.at[row, e],
                      chan=other)

    def repeat(act, e, to):
        for row in range(4):
            v = act[row, e * C:(e + 1) * C]
            for at in to:
                act[row, at * C:(at + 1) * C] = v

    def clear_edges(act):
        for side, row in ((has_down, 0), (has_up, 3)):
            @pl.when(jnp.logical_not(side))
            def _(row=row):
                act[row] = jnp.zeros(act.shape[1:], BF16)

    def conv(act, wt, o):
        acc = None
        at = pl.ds(pl.multiple_of(o * C, C), 3 * C)
        taps = [act[row, at] for row in range(4)]
        for j in range(3):
            part = jnp.dot(wt[j], jnp.concatenate(taps[j:j + 2], axis=1), preferred_element_type=F32)
            acc = part if acc is None else acc + part
        lane = iota((local, wide), 1)
        result = []
        for r in range(2):
            a = [acc[k * local:(k + 1) * local, r * wide:(r + 1) * wide] for k in range(3)]
            left = jnp.where(lane == 0, 0.0, pltpu.roll(a[0], 1, 1))
            right = jnp.where(lane == wide - 1, 0.0, pltpu.roll(a[2], wide - 1, 1))
            result.append(a[1] + left + right)
        return result

    pl.semaphore_wait(barrier, blocks * tiles)

    for s in reversed(before):
        for f in (0, 1):
            for r in (0, 1):
                go(tm + (2 - s) < blocks,
                   lat_copy(latent.at[f, r], s, 1 + r, f, x_send.at[s, r, f], tm=tm + (2 - s)))
    for f in (0, 1):
        go(has_up, lat_copy(latent.at[f, 1], 2, 0, f, z_send.at[2, 0, f], tile=tile + 1))
        go(has_down, lat_copy(latent.at[f, 0], 2, 3, f, z_send.at[2, 1, f], tile=tile - 1))

    for copy in loads:
        copy.wait()
    make_stats(0, lambda f, r: lat[2, f, 1 + r].astype(F32))
    send_stats(0)

    clear_edges(act1)
    clear_edges(act2)
    for i, factor in enumerate((0.5, 0.5, 0.5, 0.5, 1.0, 1.0)):
        cols[i] = jnp.broadcast_to(column(factor * params[i], local), (local, 128))
    a, b = iota((2 * wide, 2 * wide), 0), iota((2 * wide, 2 * wide), 1)
    select[...] = jnp.where(b == 2 * (a % wide) + a // wide, 1.0, 0.0).astype(BF16)
    load1.wait()
    flip(w1v, w1t)
    load2.wait()
    flip(w2v, w2t)

    def arrived(s, row, f):
        lat_copy(lat.at[s, f, row], s, row, f, z_send.at[2, 0, 0], tile=tile).wait_recv()

    for s in reversed(before):
        here = tm >= 2 - s
        for f in (0, 1):
            for r in (0, 1):
                when(here, functools.partial(arrived, s, 1 + r, f))
                side, row, to = ((has_down, 3, tile - 1), (has_up, 0, tile + 1))[r]
                go(jnp.logical_and(here, side),
                   lat_copy(lat.at[s, f, 1 + r], s, row, f, z_send.at[s, 1 - r, f], tile=to))

    wait_stats(0)
    make_norms(0, 6 - 2 * len(slots), 6, 0, 1, None)

    def norm1(s, f, row):
        e = 2 * s + f
        normed(act1, d_send, d_recv, e, row, lat[s, f, row].astype(F32))

    def norm1_inner(s):
        def one(step, carry):
            norm1(s, step // 2, 1 + step % 2)
            return carry

        lax.fori_loop(0, 4, one, 0)

    norm1_inner(2)
    for s in before:
        when(tm >= 2 - s, functools.partial(norm1_inner, s))

    for s in reversed(slots):
        for f in (0, 1):
            for row in (0, 3):
                @pl.when(jnp.logical_and(tm >= 2 - s, row_here(row)))
                def _(s=s, f=f, row=row):
                    arrived(s, row, f)
                    norm1(s, f, row)

    def frames1(action):
        for s in reversed(slots):
            for f in (0, 1):
                for row in (1, 2, 0, 3):
                    when(jnp.logical_and(tm >= 2 - s, row_here(row)),
                        lambda e=2 * s + f, row=row: action(of_other(act1, d_send, d_recv, e, row)))

    frames1(lambda copy: copy.wait_recv())

    when(tm == 0, lambda: repeat(act1, 4, (3, 2)))
    when(tm == 1, lambda: repeat(act1, 2, (1, 0)))

    def z_copy(o, up):
        at, r, to = (0, 1, tile + 1) if up else (1, 0, tile - 1)
        return remote(hsend.at[r, o], hedge.at[at, o], hz_send.at[at, o], h_recv.at[at, o], tile=to)

    def conv1(o, carry):
        for r, h in enumerate(conv(act1, w1t, o)):
            hid[o, r] = h
            hsend[r, o] = h.astype(BF16)

        when(has_up, lambda: z_copy(o, True).start())
        when(has_down, lambda: z_copy(o, False).start())
        return carry

    lax.fori_loop(2, 4, conv1, 0)
    make_stats(1, lambda f, r: hid[2 + f, r] + cols[4])
    send_stats(1)
    when(tm > 0, lambda: lax.fori_loop(0, 2, conv1, 0))

    wait_stats(1)
    make_norms(1, 0, 4, 2, 3, 4)

    def norm2_inner(first, steps):
        def one(step, carry):
            o, r = first + step // 2, step % 2
            normed(act2, e_send, e_recv, o, 1 + r, hid[o, r])
            return carry

        lax.fori_loop(0, steps, one, 0)

    def made(o):
        return always if o >= 2 else tm > 0

    norm2_inner(2, 4)
    when(tm > 0, lambda: norm2_inner(0, 4))

    for o in (2, 3, 0, 1):
        for at, row in ((0, 0), (1, 3)):
            @pl.when(jnp.logical_and(made(o), row_here(row)))
            def _(o=o, at=at, row=row):
                remote(hsend.at[at, o], hedge.at[at, o], hz_send.at[at, o], h_recv.at[at, o], tile=tile).wait_recv()
                normed(act2, e_send, e_recv, o, row, hedge[at, o].astype(F32))

    def frames2(action):
        for o in (2, 3, 0, 1):
            for row in (1, 2, 0, 3):
                when(jnp.logical_and(made(o), row_here(row)),
                    lambda o=o, row=row: action(of_other(act2, e_send, e_recv, o, row)))

    frames2(lambda copy: copy.wait_recv())
    when(tm == 0, lambda: repeat(act2, 2, (1, 0)))

    def conv2(o, carry):
        for r, h in enumerate(conv(act2, w2t, o)):
            mix[o * 2 + r] = lat[2, o, 1 + r].astype(F32) + (h + cols[5])
        return carry

    lax.fori_loop(0, 2, conv2, 0)

    spread = select[...]
    for f in range(2):
        for r in range(2):
            for p in range(2):
                pair = [mix[f * 2 + r, pl.ds(2 * p + q, local // 4, stride=4), :].astype(BF16) for q in range(2)]
                out[f, 2 * r + p] = jnp.dot(
                    jnp.concatenate(pair, axis=1), spread, preferred_element_type=F32
                ).astype(BF16)

    for condition, copy in started:
        @pl.when(condition)
        def _(copy=copy):
            copy.wait_send()

    for o in range(4):
        for up, side in ((True, has_up), (False, has_down)):
            when(jnp.logical_and(made(o), side), lambda o=o, up=up: z_copy(o, up).wait_send())
    frames1(lambda copy: copy.wait_send())
    frames2(lambda copy: copy.wait_send())
    for which in (0, 1):
        for b in range(blocks):
            when(b >= tm, lambda b=b, which=which: each_peer(b, lambda t: stats_to(which, b, t).wait_send()))


def shards(tiles, blocks, latent, n1g, n1b, w1, c1b, n2g, n2b, w2, c2b):
    frames, rows, local, wide = latent.shape
    count = tiles * blocks
    vmem = pl.BlockSpec(memory_space=pltpu.VMEM)
    hbm = pl.BlockSpec(memory_space=pl.ANY)
    dma = pltpu.SemaphoreType.DMA
    here = lambda v: pltpu.with_memory_space_constraint(v, pltpu.HBM)
    row = lambda v: here(v.reshape(1, local))
    return pl.pallas_call(
        functools.partial(kernel, tiles, blocks),
        out_shape=jax.ShapeDtypeStruct((frames, 2 * rows, local // 4, 2 * wide), BF16),
        in_specs=[hbm] * 9,
        out_specs=vmem,
        scratch_shapes=[
            pltpu.VMEM(w1.shape, BF16),
            pltpu.VMEM(w2.shape, BF16),
            pltpu.VMEM((3, 3 * local, 3 * C), BF16),
            pltpu.VMEM((3, 3 * local, 3 * C), BF16),
            pltpu.VMEM((3, 2, 4, local, wide), BF16),
            pltpu.VMEM((4, 6 * C, wide), BF16),
            pltpu.VMEM((4, 2, local, wide), F32),
            pltpu.VMEM((2, 4, local, wide), BF16),
            pltpu.VMEM((2, 4, local, wide), BF16),
            pltpu.VMEM((4, 4 * C, wide), BF16),
            pltpu.VMEM((4, local, wide), F32),
            pltpu.VMEM((2 * wide, 2 * wide), BF16),
            pltpu.VMEM((6, 1, local), F32),
            pltpu.VMEM((6, local, 128), F32),
            pltpu.VMEM((6, 2, local, 128), F32),
            pltpu.VMEM((2, 1, 128), F32),
            pltpu.VMEM((2, count, 1, 128), F32),
            dma((7,)),
            dma((2,)),
            dma((2, 2, 2)),
            dma((3, 2, 2)),
            dma((3, 4, 2)),
            dma((4, 6)),
            dma((4, 6)),
            dma((2, 4)),
            dma((2, 4)),
            dma((4, 4)),
            dma((4, 4)),
            dma((2, count)),
            dma((2, count)),
        ],
        compiler_params=pltpu.CompilerParams(
            collective_id=0, has_side_effects=True, vmem_limit_bytes=48 * 1024 * 1024
        ),
        name="block",
    )(here(latent), row(n1g), row(n1b), here(w1), row(c1b), row(n2g), row(n2b), here(w2), row(c2b))


def solution(mesh):
    return jax.shard_map(
        functools.partial(shards, mesh.shape["tile"], mesh.shape["tm"]),
        mesh=mesh,
        in_specs=(
            P(("clip", "tm"), "tile", "chan", None),
            P("chan"),
            P("chan"),
            P(None, None, None, None, "chan"),
            P("chan"),
            P("chan"),
            P("chan"),
            P(None, None, None, None, "chan"),
            P("chan"),
        ),
        out_specs=P(("clip", "tm"), "tile", "chan", None),
        check_vma=False,
    )
```

time: 27.6 us -> 23.3 us (0.84)
  Pallas kernels: 26.7 us -> 22.5 us
    pallas_call x1, Pallas kernels: 26.7 us -> 22.5 us  [shards(): pl.pallas_call(functools.partial(kernel, tiles, blocks), out_shape=jax.Sh...]
where the time goes in v1:
time: 23.3 us; the launch traced here: 23.2 us
  Pallas kernels  22.5 us (97%)
  local copies, waits for them, and re-layouts  0.66 us (3%)
    pallas_call x1, Pallas kernels, shards(): pl.pallas_call(functools.partial(kernel, tiles, blocks), out_shape=jax.Sh...  22.5 us
    unnamed x1, local copies, waits for them, and re-layouts  0.66 us

profile of v1, /device:TPU:3, one launch (start us, length us, event | category | flops | bytes accessed | tf_op | source)
XLA Modules:
  0.0 23.2 jit_solution(14224266816997834480)
XLA Ops:
  0.0 22.5 %block.1 = bf16[2,4,32,256]{3,2,1,0:T(8,128)(2,1)S(1)} custom-call(bf16[2,2,128,128]{3,2,1,0:T(8,128)(2,1)} %latent.1, f32[1,128]{1,0:T(1,128)} %bitcast.6, f32[1,128]{1,0:T(1,128)} %bitcast.7, bf16[3,3,3,256,128]{4,3,2,1,0:T(8,128)(2,1)} %w1.1, f32[1,128]{1,0:T(1,128)} %bitcast.8, f32[1,128]{1,0:T(1,128)} %bitcast.9, f32[1,128]{1,0:T(1,128)} %bitcast.10, ...), custom_call_target="tpu_custom_call" | custom-call | tf_op jit(solution)/shard_map/block/pallas_call | solution.py:423
  22.5 0.7 %copy.11 = bf16[2,4,32,256]{3,2,1,0:T(8,128)(2,1)} copy(bf16[2,4,32,256]{3,2,1,0:T(8,128)(2,1)S(1)} %block.1) | data formatting | bytes 262144
